TPU v7x, 32 devices: a whole 2x2x4 slice. The times are simulated.
32 devices in a mesh: wide: 8 (over z, y), narrow: 4 (over x, core).
Axes of the slice: x: 2, y: 2, z: 4, core: 2. Of those that a mesh axis runs over, the one named last changes fastest.
Arguments:
- frames: bfloat16 [256, 2, 256, 256], P(('wide', 'narrow')), may hold values from -120 to 120
- sketch: bfloat16 [256, 128], replicated, may hold values from -0.3 to 2.3
- kernel_taps: bfloat16 [64], replicated, may hold values from -0.3 to 1.1
Outputs:
- basis: float32 [128, 32768], P(None, ('wide', 'narrow'))
- factor: float32 [128, 128], replicated
All inputs are finite; a program needn't handle non-finite values.
Results may differ from a plain program's by a relative error of at most 0.0043.
Values may be sent and summed in bfloat16 or wider, within the bound.
No kernel may reach another device: no remote copies, remote signals or barrier semaphores. Data moves between devices by JAX's collectives and lax.ppermute only.
A program may use at most 64 MiB of HBM per device.

v0:
```python
import jax
import jax.numpy as jnp
from jax import lax
from jax.sharding import PartitionSpec as P


def gauss_taps(spread):
    position = jnp.arange(15, dtype=jnp.float32) - 7.0
    weights = jnp.exp(-position * position / (2.0 * spread * spread))
    return weights / jnp.sum(weights)


def band_matrix(spread, length):
    outputs = length // 2
    offset_index = (
        jnp.arange(length, dtype=jnp.int32)[None, :]
        - 2 * jnp.arange(outputs, dtype=jnp.int32)[:, None]
        + 7
    )
    weights = gauss_taps(spread)
    matrix = jnp.zeros((outputs, length), jnp.float32)
    for offset in range(15):
        matrix = matrix + jnp.where(offset_index == offset, weights[offset], jnp.float32(0.0))
    return matrix


def filter_volumes(frames_block):
    volume = frames_block.astype(jnp.float32)
    row_count = volume.shape[-2]
    col_count = volume.shape[-1]
    half = col_count // 2
    column_bands = jnp.concatenate(
        [band_matrix(1.5, col_count), band_matrix(3.0, col_count)], axis=0
    )
    column_pass = jnp.einsum(
        "...rc,oc->...ro", volume, column_bands, precision=lax.Precision.HIGHEST
    )
    narrow_pass = jnp.einsum(
        "or,...rc->...oc",
        band_matrix(1.5, row_count),
        column_pass[..., :half],
        precision=lax.Precision.HIGHEST,
    )
    broad_pass = jnp.einsum(
        "or,...rc->...oc",
        band_matrix(3.0, row_count),
        column_pass[..., half:],
        precision=lax.Precision.HIGHEST,
    )
    return (narrow_pass - broad_pass).astype(jnp.bfloat16)


def build_toeplitz(kernel_taps, length):
    lag_index = (
        jnp.arange(length, dtype=jnp.int32)[:, None] - jnp.arange(length, dtype=jnp.int32)[None, :]
    )
    toeplitz = jnp.zeros((length, length), jnp.float32)
    for offset in range(kernel_taps.shape[0]):
        toeplitz = toeplitz + jnp.where(
            lag_index == offset, kernel_taps[offset].astype(jnp.float32), jnp.float32(0.0)
        )
    return toeplitz.astype(jnp.bfloat16)


def high_dot(left, right):
    return jnp.dot(left, right, precision=lax.Precision.HIGHEST, preferred_element_type=jnp.float32)


def shards(frames, sketch, kernel_taps):
    filtered = filter_volumes(frames)
    per_device = frames.shape[0]
    flattened = filtered.reshape(per_device, -1)
    voxel_count = flattened.shape[1]
    group_size = lax.axis_size(("wide", "narrow"))
    block = voxel_count // group_size
    length = per_device * group_size
    toeplitz = build_toeplitz(kernel_taps, length)
    arranged = flattened.reshape(1, per_device, group_size, block)
    received = lax.all_to_all(arranged, ("wide", "narrow"), split_axis=2, concat_axis=0, tiled=True)
    deconvolved = jnp.dot(
        toeplitz, received.reshape(length, received.shape[3]), preferred_element_type=jnp.float32
    ).astype(jnp.bfloat16)
    sketched = lax.dot_general(
        sketch, deconvolved, (((0,), (0,)), ((), ())), preferred_element_type=jnp.float32
    )
    deconvolved, sketched = (deconvolved, sketched)
    series = deconvolved.astype(jnp.float32)
    local_gram = (
        lax.dot_general(
            deconvolved, deconvolved, (((1,), (1,)), ((), ())), preferred_element_type=jnp.float32
        )
        / voxel_count
    )
    data_gram = lax.psum(local_gram, ("wide", "narrow"))
    sketch_full = sketch.astype(jnp.float32)
    weighted = high_dot(data_gram, sketch_full)
    first_lower = jnp.linalg.cholesky(high_dot(sketch_full.T, weighted))
    projected = jax.scipy.linalg.solve_triangular(first_lower, weighted.T, lower=True).T
    second_lower = jnp.linalg.cholesky(high_dot(projected.T, high_dot(data_gram, projected)))
    combined = jax.scipy.linalg.solve_triangular(second_lower, projected.T, lower=True)
    basis = high_dot(combined, series)
    factor = second_lower.T
    return (basis, factor)


def solution(mesh):
    return jax.shard_map(
        shards,
        mesh=mesh,
        in_specs=(P(("wide", "narrow"), None, None, None), P(), P()),
        out_specs=(P(None, ("wide", "narrow")), P()),
        check_vma=False,
    )
```

profile of v0, /device:TPU:0, one launch (start us, length us, event | category | flops | bytes accessed | tf_op | source)
XLA Modules:
  0.0 296.3 jit_solution(4108505157623894362)
XLA Ops:
  7.2 0.0 copy-start
  7.2 0.6 fusion.237
  7.8 0.6 fusion.238
  8.4 0.7 broadcast_divide_fusion.1
  9.1 0.7 fusion.341
  9.8 0.7 broadcast_divide_fusion
  10.4 0.7 fusion.342
  11.1 9.6 %select_add_fusion.1 = f32[128,256]{1,0:T(8,128)S(1)} fusion(f32[]{:T(128)} %bitcast.78, f32[]{:T(128)} %bitcast.77, f32[]{:T(128)} %bitcast.76, f32[]{:T(128)} %bitcast.75, f32[]{:T(128)} %bitcast.74, f32[]{:T(128)} %bitcast.73, f32[]{:T(128)} %bitcast.72, f32[]{:T(128)} %bitcast.71, f32[]{:T(128)} %bitcast.70, f32[]{:T(128)} %bitcast.69, f32[]{:T(128)} %bitcast.68, ...), kind=kLoop, calls=%fused_computation.85 | loop fusion | flops 1507328 | bytes 131644 | tf_op jit(solution)/shard_map/add | solution.py:23
  20.7 9.7 %select_add_fusion = f32[128,256]{1,0:T(8,128)S(1)} fusion(f32[]{:T(128)} %bitcast.93, f32[]{:T(128)} %bitcast.92, f32[]{:T(128)} %bitcast.91, f32[]{:T(128)} %bitcast.90, f32[]{:T(128)} %bitcast.89, f32[]{:T(128)} %bitcast.88, f32[]{:T(128)} %bitcast.87, f32[]{:T(128)} %bitcast.86, f32[]{:T(128)} %bitcast.85, f32[]{:T(128)} %bitcast.84, f32[]{:T(128)} %bitcast.83, ...), kind=kLoop, calls=%fused_computation.84 | loop fusion | flops 1507328 | bytes 131644 | tf_op jit(solution)/shard_map/add | solution.py:23
  30.4 0.0 copy-done
  30.4 1.9 convolution_bitcast_fusion
  32.3 11.5 %fusion = f32[8,2,128,128]{3,2,1,0:T(8,128)S(1)} fusion(f32[8,2,256,256]{2,3,1,0:T(8,128)S(1)} %convolution_bitcast_fusion, f32[]{:T(128)} %bitcast.93, f32[]{:T(128)} %bitcast.92, f32[]{:T(128)} %bitcast.91, f32[]{:T(128)} %bitcast.90, f32[]{:T(128)} %bitcast.89, f32[]{:T(128)} %bitcast.88, f32[]{:T(128)} %bitcast.87, f32[]{:T(128)} %bitcast.86, ...), kind=kOutput, calls=%fused_computation.1 | convolution fusion | flops 806813696 | bytes 3146300 | tf_op jit(solution)/shard_map/or,...rc->...oc/dot_general | solution.py:44
  43.8 11.4 %fusion.10 = bf16[8,2,128,128]{2,3,1,0:T(8,128)(2,1)S(1)} fusion(f32[8,2,128,128]{3,2,1,0:T(8,128)S(1)} %fusion, f32[8,2,256,256]{2,3,1,0:T(8,128)S(1)} %convolution_bitcast_fusion, f32[]{:T(128)} %bitcast.78, f32[]{:T(128)} %bitcast.77, f32[]{:T(128)} %bitcast.76, f32[]{:T(128)} %bitcast.75, f32[]{:T(128)} %bitcast.74, f32[]{:T(128)} %bitcast.73, ...), kind=kOutput, calls=%fused_computation.8 | convolution fusion | flops 807337984 | bytes 3670588 | tf_op jit(solution)/shard_map/or,...rc->...oc/dot_general | solution.py:38
  55.2 0.0 copy-start.1
  55.2 0.3 copy.13
  55.5 0.2 reshape_reshape.3
  55.7 1.1 copy.14
  56.8 7.3 %all-to-all-start = ((bf16[1,8,32,1024]{3,1,0,2:T(8,128)(2,1)}), bf16[1,8,32,1024]{3,1,0,2:T(8,128)(2,1)S(1)}, u32[]{:S(2)}, u32[]{:S(2)}) async-start(bf16[1,8,32,1024]{3,1,0,2:T(8,128)(2,1)} %copy.14), calls=%async_computation | async-start | bytes 1048576 | tf_op jit(solution)/shard_map/all_to_all | solution.py:79
  64.2 0.2 all-reduce.2.cloned.1.call-start
  64.4 0.0 copy-done.1
  64.4 0.7 fusion.338
  70.2 0.7 fusion.337
  83.5 0.7 fusion.339
  102.4 0.7 fusion.340
  107.5 0.0 copy-start.2
  107.5 0.0 all-to-all-done
  107.5 1.1 convolution_convert_fusion
  108.6 1.0 convolution_multiply_fusion
  109.6 0.0 all-reduce.2.cloned.1.call-update
  109.7 128.0 %all-reduce.2.cloned.1.call-done = f32[256,256]{1,0:T(8,128)} async-done(((f32[256,256]{1,0:T(8,128)}), f32[256,256]{1,0:T(8,128)}) %all-reduce.2.cloned.1.call-update) | async-done | bytes 262160 | tf_op jit(solution)/shard_map/psum | solution.py:94
  237.7 0.0 copy-done.2
  237.7 1.2 fusion.343
  238.9 0.3 fusion.344
  239.2 0.1 copy.15
  239.3 11.7 %cholesky.44 = f32[128,128]{1,0:T(8,128)S(1)} custom-call(f32[128,128]{1,0:T(8,128)S(1)} %add_multiply_fusion), custom_call_target="Cholesky" | custom-call | tf_op jit(solution)/shard_map/jit(cholesky)/cholesky | solution.py:97
  251.1 0.6 compare_reduce_fusion.1
  251.7 0.7 fusion.228
  252.4 9.8 %custom-call.6 = f32[1,128,128]{1,2,0:T(8,128)S(1)} custom-call(f32[1,128,128]{2,1,0:T(8,128)S(1)} %fusion.228), custom_call_target="InvertDiagBlocksLowerTriangular" | custom-call | tf_op jit(solution)/shard_map/jit(_solve_triangular)/triangular_solve | solution.py:98
  262.2 0.3 fusion.82
  262.5 1.3 fusion.345
  263.8 0.3 fusion.346
  264.1 0.1 copy.16
  264.2 11.9 %cholesky.55 = f32[128,128]{1,0:T(8,128)S(1)} custom-call(f32[128,128]{1,0:T(8,128)S(1)} %fusion.231), custom_call_target="Cholesky" | custom-call | tf_op jit(solution)/shard_map/jit(cholesky)/cholesky | solution.py:99
  276.1 0.6 compare_reduce_fusion
  276.8 0.7 fusion.236
  277.4 9.8 %custom-call.7 = f32[1,128,128]{1,2,0:T(8,128)S(1)} custom-call(f32[1,128,128]{2,1,0:T(8,128)S(1)} %get-tuple-element.11), custom_call_target="InvertDiagBlocksLowerTriangular" | custom-call | tf_op jit(solution)/shard_map/jit(_solve_triangular)/triangular_solve | solution.py:100
  287.3 0.3 fusion.229
  287.6 1.2 fusion.347
  288.7 0.7 copy.17
  (5 shorter events, 0.1 us)
Async XLA Ops:
  7.2 23.2 %copy-start = (bf16[8,2,256,256]{3,2,1,0:T(8,128)(2,1)S(1)}, bf16[8,2,256,256]{3,2,1,0:T(8,128)(2,1)}, u32[]{:S(2)}) copy-start(bf16[8,2,256,256]{3,2,1,0:T(8,128)(2,1)} %param.6) | copy-start | bytes 6291460
  55.2 9.2 %copy-start.1 = (bf16[64]{0:T(256)(128)(2,1)S(1)}, bf16[64]{0:T(256)(128)(2,1)}, u32[]{:S(2)}) copy-start(bf16[64]{0:T(256)(128)(2,1)} %param.8) | copy-start | bytes 388
  56.8 50.7 %all-to-all-start = ((bf16[1,8,32,1024]{3,1,0,2:T(8,128)(2,1)}), bf16[1,8,32,1024]{3,1,0,2:T(8,128)(2,1)S(1)}, u32[]{:S(2)}, u32[]{:S(2)}) async-start(bf16[1,8,32,1024]{3,1,0,2:T(8,128)(2,1)} %copy.14), calls=%async_computation | async-start | bytes 1048576 | tf_op jit(solution)/shard_map/all_to_all | solution.py:79
  64.2 173.5 %all-reduce.2.cloned.1.call-start = ((), (), s32[]{:S(2)}) async-start(), calls=%async_computation.1 | async-start | bytes 524288 | tf_op jit(solution)/shard_map/psum | solution.py:94
  107.5 130.2 %copy-start.2 = (bf16[256,128]{1,0:T(8,128)(2,1)S(1)}, bf16[256,128]{1,0:T(8,128)(2,1)}, u32[]{:S(2)}) copy-start(bf16[256,128]{1,0:T(8,128)(2,1)} %param.7) | copy-start | bytes 196612
Sparse Core Ops, SparseCore 0:
  109.8 127.8 all-reduce.1
where the time goes:
time: 298 us; the launch traced here: 296 us
  waiting for transfers between devices  128 us (43%)
  other arithmetic  67.7 us (23%)
  between operations  54.4 us (18%)
  matrix products  31.8 us (11%)
  starting transfers between devices  7.54 us (3%)
  local copies, waits for them, and re-layouts  6.83 us (2%)
    psum x1, waiting for transfers between devices, shards(): data_gram = lax.psum(local_gram, ('wide', 'narrow'))  128 us
    add x2, other arithmetic, band_matrix(): matrix + jnp.where(offset_index == offset, weights[offset], jnp.float32(0...  19.2 us
    another operation x3, other arithmetic, shards(): jnp.linalg.cholesky(high_dot(projected.T, high_dot(data_gram, projected)))  12.6 us
    another operation x3, other arithmetic, shards(): first_lower = jnp.linalg.cholesky(high_dot(sketch_full.T, weighted))  12.4 us
    dot_general x1, matrix products, filter_volumes(): jnp.einsum('or,...rc->...oc', band_matrix(3.0, row_count), column_pass[.....  11.5 us
    dot_general x1, matrix products, filter_volumes(): jnp.einsum('or,...rc->...oc', band_matrix(1.5, row_count), column_pass[.....  11.4 us
    another operation x2, other arithmetic, shards(): jax.scipy.linalg.solve_triangular(first_lower, weighted.T, lower=True)  10.5 us
    another operation x1, other arithmetic, shards(): jax.scipy.linalg.solve_triangular(second_lower, projected.T, lower=True)  9.81 us
  transfers between devices with their start and end apart: 2, of which 1 were waited for; matrix products, arithmetic and copies ran while one was open for 1% of the time, Pallas kernels for 0%

commit v1 on v0

--- a/solution.py
+++ b/solution.py
@@ -2,6 +2,16 @@
 import jax.numpy as jnp
 from jax import lax
 from jax.sharding import PartitionSpec as P
+
+sites_launch = lambda frame, axis_name, out_dim, join_dim: jnp.concatenate(
+    lax.all_to_all(
+        jnp.stack(jnp.split(frame, lax.axis_size(axis_name), axis=out_dim), 0),
+        axis_name=axis_name,
+        split_axis=0,
+        concat_axis=0,
+    ),
+    axis=join_dim,
+)
 
 
 def gauss_taps(spread):
@@ -76,7 +86,7 @@
     length = per_device * group_size
     toeplitz = build_toeplitz(kernel_taps, length)
     arranged = flattened.reshape(1, per_device, group_size, block)
-    received = lax.all_to_all(arranged, ("wide", "narrow"), split_axis=2, concat_axis=0, tiled=True)
+    received = sites_launch(arranged, ("wide", "narrow"), 2, 0)
     deconvolved = jnp.dot(
         toeplitz, received.reshape(length, received.shape[3]), preferred_element_type=jnp.float32
     ).astype(jnp.bfloat16)

time: 298 us -> 317 us (1.064)
  local copies, waits for them, and re-layouts: 6.83 us -> 26.5 us
    unnamed x7 -> x38, local copies, waits for them, and re-layouts: 0.75 us -> 19.7 us
where the time goes in v1:
time: 317 us; the launch traced here: 316 us
  waiting for transfers between devices  128 us (40%)
  other arithmetic  67.7 us (21%)
  between operations  54.5 us (17%)
  matrix products  31.8 us (10%)
  local copies, waits for them, and re-layouts  26.5 us (8%)
  starting transfers between devices  7.54 us (2%)
    psum x1, waiting for transfers between devices, shards(): data_gram = lax.psum(local_gram, ('wide', 'narrow'))  128 us
    unnamed x38, local copies, waits for them, and re-layouts  19.7 us
    add x2, other arithmetic, band_matrix(): matrix + jnp.where(offset_index == offset, weights[offset], jnp.float32(0...  19.2 us
    another operation x3, other arithmetic, shards(): jnp.linalg.cholesky(high_dot(projected.T, high_dot(data_gram, projected)))  12.6 us
    another operation x3, other arithmetic, shards(): first_lower = jnp.linalg.cholesky(high_dot(sketch_full.T, weighted))  12.4 us
    dot_general x1, matrix products, filter_volumes(): jnp.einsum('or,...rc->...oc', band_matrix(3.0, row_count), column_pass[.....  11.5 us
    dot_general x1, matrix products, filter_volumes(): jnp.einsum('or,...rc->...oc', band_matrix(1.5, row_count), column_pass[.....  11.4 us
    another operation x2, other arithmetic, shards(): jax.scipy.linalg.solve_triangular(first_lower, weighted.T, lower=True)  10.5 us
  transfers between devices with their start and end apart: 2, of which 1 were waited for; matrix products, arithmetic and copies ran while one was open for 1% of the time, Pallas kernels for 0%

profile of v1, /device:TPU:0, one launch (start us, length us, event | category | flops | bytes accessed | tf_op | source)
XLA Modules:
  0.0 316.0 jit_solution(10308475412119456054)
XLA Ops:
  7.2 0.6 fusion.237
  7.8 0.6 fusion.238
  8.4 0.7 broadcast_divide_fusion.1
  9.1 0.7 fusion.343
  9.8 0.7 broadcast_divide_fusion
  10.4 0.7 fusion.344
  11.1 9.6 %select_add_fusion.1 = f32[128,256]{1,0:T(8,128)S(1)} fusion(f32[]{:T(128)} %bitcast.78, f32[]{:T(128)} %bitcast.77, f32[]{:T(128)} %bitcast.76, f32[]{:T(128)} %bitcast.75, f32[]{:T(128)} %bitcast.74, f32[]{:T(128)} %bitcast.73, f32[]{:T(128)} %bitcast.72, f32[]{:T(128)} %bitcast.71, f32[]{:T(128)} %bitcast.70, f32[]{:T(128)} %bitcast.69, f32[]{:T(128)} %bitcast.68, ...), kind=kLoop, calls=%fused_computation.85 | loop fusion | flops 1507328 | bytes 131644 | tf_op jit(solution)/shard_map/add | solution.py:33
  20.7 9.7 %select_add_fusion = f32[128,256]{1,0:T(8,128)S(1)} fusion(f32[]{:T(128)} %bitcast.93, f32[]{:T(128)} %bitcast.92, f32[]{:T(128)} %bitcast.91, f32[]{:T(128)} %bitcast.90, f32[]{:T(128)} %bitcast.89, f32[]{:T(128)} %bitcast.88, f32[]{:T(128)} %bitcast.87, f32[]{:T(128)} %bitcast.86, f32[]{:T(128)} %bitcast.85, f32[]{:T(128)} %bitcast.84, f32[]{:T(128)} %bitcast.83, ...), kind=kLoop, calls=%fused_computation.84 | loop fusion | flops 1507328 | bytes 131644 | tf_op jit(solution)/shard_map/add | solution.py:33
  30.4 1.9 convolution_bitcast_fusion
  32.3 11.5 %fusion = f32[8,2,128,128]{3,2,1,0:T(8,128)S(1)} fusion(f32[8,2,256,256]{2,3,1,0:T(8,128)S(1)} %convolution_bitcast_fusion, f32[]{:T(128)} %bitcast.93, f32[]{:T(128)} %bitcast.92, f32[]{:T(128)} %bitcast.91, f32[]{:T(128)} %bitcast.90, f32[]{:T(128)} %bitcast.89, f32[]{:T(128)} %bitcast.88, f32[]{:T(128)} %bitcast.87, f32[]{:T(128)} %bitcast.86, ...), kind=kOutput, calls=%fused_computation.1 | convolution fusion | flops 806813696 | bytes 3146300 | tf_op jit(solution)/shard_map/or,...rc->...oc/dot_general | solution.py:54
  43.8 11.4 %fusion.10 = bf16[8,2,128,128]{2,3,1,0:T(8,128)(2,1)S(1)} fusion(f32[8,2,128,128]{3,2,1,0:T(8,128)S(1)} %fusion, f32[8,2,256,256]{2,3,1,0:T(8,128)S(1)} %convolution_bitcast_fusion, f32[]{:T(128)} %bitcast.78, f32[]{:T(128)} %bitcast.77, f32[]{:T(128)} %bitcast.76, f32[]{:T(128)} %bitcast.75, f32[]{:T(128)} %bitcast.74, f32[]{:T(128)} %bitcast.73, ...), kind=kOutput, calls=%fused_computation.8 | convolution fusion | flops 807337984 | bytes 3670588 | tf_op jit(solution)/shard_map/or,...rc->...oc/dot_general | solution.py:48
  56.2 0.7 fusion.337
  56.9 0.6 constant_dynamic-update-slice_fusion.31
  57.5 0.6 constant_dynamic-update-slice_fusion.30
  58.1 0.6 constant_dynamic-update-slice_fusion.29
  58.7 0.6 constant_dynamic-update-slice_fusion.28
  59.3 0.6 constant_dynamic-update-slice_fusion.27
  60.0 0.6 constant_dynamic-update-slice_fusion.26
  60.6 0.6 constant_dynamic-update-slice_fusion.25
  61.2 0.6 constant_dynamic-update-slice_fusion.24
  61.8 0.6 constant_dynamic-update-slice_fusion.23
  62.4 0.6 constant_dynamic-update-slice_fusion.22
  63.0 0.6 constant_dynamic-update-slice_fusion.21
  63.6 0.6 constant_dynamic-update-slice_fusion.20
  64.2 0.6 constant_dynamic-update-slice_fusion.19
  64.9 0.6 constant_dynamic-update-slice_fusion.18
  65.5 0.6 constant_dynamic-update-slice_fusion.17
  66.1 0.6 constant_dynamic-update-slice_fusion.16
  66.7 0.6 constant_dynamic-update-slice_fusion.15
  67.3 0.6 constant_dynamic-update-slice_fusion.14
  67.9 0.6 constant_dynamic-update-slice_fusion.13
  68.5 0.6 constant_dynamic-update-slice_fusion.12
  69.1 0.6 constant_dynamic-update-slice_fusion.11
  69.8 0.6 constant_dynamic-update-slice_fusion.10
  70.4 0.6 constant_dynamic-update-slice_fusion.9
  71.0 0.6 constant_dynamic-update-slice_fusion.8
  71.6 0.6 constant_dynamic-update-slice_fusion.7
  72.2 0.6 constant_dynamic-update-slice_fusion.6
  72.8 0.6 constant_dynamic-update-slice_fusion.5
  73.4 0.6 constant_dynamic-update-slice_fusion.4
  74.1 0.6 constant_dynamic-update-slice_fusion.3
  74.7 0.6 constant_dynamic-update-slice_fusion.2
  75.3 0.6 constant_dynamic-update-slice_fusion.1
  75.9 0.6 constant_dynamic-update-slice_fusion
  76.5 7.3 %all-to-all-start = ((bf16[32,1,8,1,1024]{4,2,3,1,0:T(8,128)(2,1)}), bf16[32,1,8,1,1024]{4,2,3,1,0:T(8,128)(2,1)S(1)}, u32[]{:S(2)}, u32[]{:S(2)}) async-start(bf16[32,1,8,1,1024]{4,2,3,1,0:T(8,128)(2,1)} %constant_dynamic-update-slice_fusion), calls=%async_computation | async-start | bytes 1048576 | tf_op jit(solution)/shard_map/all_to_all | solution.py:7
  84.1 0.7 fusion.340
  89.8 0.7 fusion.339
  103.2 0.7 fusion.341
  122.1 0.7 fusion.342
  127.2 1.1 convolution_convert_fusion
  128.3 1.0 convolution_multiply_fusion
  129.3 128.0 %all-reduce.2.cloned.1.call-done = f32[256,256]{1,0:T(8,128)} async-done(((f32[256,256]{1,0:T(8,128)}), f32[256,256]{1,0:T(8,128)}) %all-reduce.2.cloned.1.call-update) | async-done | bytes 262160 | tf_op jit(solution)/shard_map/psum | solution.py:104
  257.4 1.2 fusion.345
  259.0 11.7 %cholesky.44 = f32[128,128]{1,0:T(8,128)S(1)} custom-call(f32[128,128]{1,0:T(8,128)S(1)} %add_multiply_fusion), custom_call_target="Cholesky" | custom-call | tf_op jit(solution)/shard_map/jit(cholesky)/cholesky | solution.py:107
  270.7 0.6 compare_reduce_fusion.1
  271.4 0.7 fusion.228
  272.0 9.8 %custom-call.6 = f32[1,128,128]{1,2,0:T(8,128)S(1)} custom-call(f32[1,128,128]{2,1,0:T(8,128)S(1)} %fusion.228), custom_call_target="InvertDiagBlocksLowerTriangular" | custom-call | tf_op jit(solution)/shard_map/jit(_solve_triangular)/triangular_solve | solution.py:108
  282.2 1.3 fusion.347
  283.9 11.9 %cholesky.55 = f32[128,128]{1,0:T(8,128)S(1)} custom-call(f32[128,128]{1,0:T(8,128)S(1)} %fusion.231), custom_call_target="Cholesky" | custom-call | tf_op jit(solution)/shard_map/jit(cholesky)/cholesky | solution.py:109
  295.8 0.6 compare_reduce_fusion
  296.5 0.7 fusion.236
  297.1 9.8 %custom-call.7 = f32[1,128,128]{1,2,0:T(8,128)S(1)} custom-call(f32[1,128,128]{2,1,0:T(8,128)S(1)} %get-tuple-element.101), custom_call_target="InvertDiagBlocksLowerTriangular" | custom-call | tf_op jit(solution)/shard_map/jit(_solve_triangular)/triangular_solve | solution.py:110
  307.2 1.2 fusion.349
  308.4 0.7 copy.627
  (23 shorter events, 2.7 us)
Async XLA Ops:
  7.2 23.2 %copy-start = (bf16[8,2,256,256]{3,2,1,0:T(8,128)(2,1)S(1)}, bf16[8,2,256,256]{3,2,1,0:T(8,128)(2,1)}, u32[]{:S(2)}) copy-start(bf16[8,2,256,256]{3,2,1,0:T(8,128)(2,1)} %param.6) | copy-start | bytes 6291460
  56.2 27.9 %copy-start.1 = (bf16[64]{0:T(256)(128)(2,1)S(1)}, bf16[64]{0:T(256)(128)(2,1)}, u32[]{:S(2)}) copy-start(bf16[64]{0:T(256)(128)(2,1)} %param.8) | copy-start | bytes 388
  76.5 50.7 %all-to-all-start = ((bf16[32,1,8,1,1024]{4,2,3,1,0:T(8,128)(2,1)}), bf16[32,1,8,1,1024]{4,2,3,1,0:T(8,128)(2,1)S(1)}, u32[]{:S(2)}, u32[]{:S(2)}) async-start(bf16[32,1,8,1,1024]{4,2,3,1,0:T(8,128)(2,1)} %constant_dynamic-update-slice_fusion), calls=%async_computation | async-start | bytes 1048576 | tf_op jit(solution)/shard_map/all_to_all | solution.py:7
  83.8 173.5 %all-reduce.2.cloned.1.call-start = ((), (), s32[]{:S(2)}) async-start(), calls=%async_computation.1 | async-start | bytes 524288 | tf_op jit(solution)/shard_map/psum | solution.py:104
  127.2 130.2 %copy-start.2 = (bf16[256,128]{1,0:T(8,128)(2,1)S(1)}, bf16[256,128]{1,0:T(8,128)(2,1)}, u32[]{:S(2)}) copy-start(bf16[256,128]{1,0:T(8,128)(2,1)} %param.7) | copy-start | bytes 196612
Sparse Core Ops, SparseCore 0:
  129.5 127.8 all-reduce.1
